TPU v7x, 512 devices: a whole 4x8x8 slice. The times are simulated.
512 devices in a mesh: expert: 64 (over z, y), tensor: 8 (over x, core).
Axes of the slice: x: 4, y: 8, z: 8, core: 2. Of those that a mesh axis runs over, the one named last changes fastest.
Arguments:
- attn_out: bfloat16 [8192, 4096], P('expert', 'tensor'), may hold values from -6 to 6
- out_weight: bfloat16 [4096, 2048], P('tensor'), may hold values from -0.09375 to 0.09375
- residual: bfloat16 [8192, 2048], P(('expert', 'tensor')), may hold values from -6 to 6
- attn_gain: float32 [2048], replicated, may hold values from 0.1 to 1.9
- expert_ids: int32 [8192, 8], P('expert'), may hold values from 0 to 127, all different within a row; in each aligned block of 128 rows (0 to 127, 128 to 255, ...) at most 12 rows name the same one
- route_weights: float32 [8192, 8], P('expert'), may hold values from 0.05 to 0.3
- w_gate: bfloat16 [64, 2048, 1536], P('expert', None, 'tensor'), may hold values from -0.125 to 0.125
- w_up: bfloat16 [64, 2048, 1536], P('expert', None, 'tensor'), may hold values from -0.125 to 0.125
- w_down: bfloat16 [64, 1536, 2048], P('expert', 'tensor'), may hold values from -0.21875 to 0.21875
- input_gain: float32 [2048], replicated, may hold values from 0.1 to 1.9
- q_weight: bfloat16 [2048, 4096], P('expert', 'tensor'), may hold values from -0.125 to 0.125
- kv_weight: bfloat16 [2048, 1024], P('expert', 'tensor'), may hold values from -0.125 to 0.125
- q_gain: float32 [128], replicated, may hold values from 0.1 to 1.9
- k_gain: float32 [128], replicated, may hold values from 0.1 to 1.9
Outputs:
- next_residual: bfloat16 [8192, 2048], P(('expert', 'tensor'))
- queries: bfloat16 [8192, 4096], P('expert', 'tensor')
- keys_values: bfloat16 [8192, 1024], P('expert', 'tensor')
Inputs may be any that keep to these rules, and one draw needn't show every extreme that they name: `expert_ids`: each row names 8 different experts. In each aligned block of 128 rows no expert is named by more than 12 rows, and in some block one expert is named by exactly 12 rows.
All inputs are finite; a program needn't handle non-finite values.
Results may differ from a plain program's by a relative error of at most 0.012.
Values may be sent and summed in bfloat16 or wider, within the bound.
A program may use at most 64 MiB of HBM per device.

v0:
```python
import jax
import jax.numpy as jnp
from jax import lax
from jax.sharding import PartitionSpec as P

KV_HEADS = 4
TOP = 8
EPSILON = 1e-06


def normalize(values, gain):
    return values * lax.rsqrt(jnp.mean(values * values, axis=-1, keepdims=True) + EPSILON) * gain


def per_device(
    attn_out,
    out_weight,
    residual,
    attn_gain,
    expert_ids,
    route_weights,
    w_gate,
    w_up,
    w_down,
    input_gain,
    q_weight,
    kv_weight,
    q_gain,
    k_gain,
):
    n_expert = lax.axis_size("expert")
    n_tensor = lax.axis_size("tensor")
    share = n_tensor // 2
    tensor_index = lax.axis_index("tensor")
    group_rows = attn_out.shape[0]
    width = residual.shape[1]
    half = tensor_index // share
    capacity = 3 * group_rows * TOP // (4 * n_expert)
    all_experts = 2 * n_expert
    attn_rows = lax.psum_scatter(
        jnp.dot(attn_out, out_weight, preferred_element_type=jnp.float32),
        "tensor",
        scatter_dimension=0,
        tiled=True,
    )
    first_residual = (residual.astype(jnp.float32) + attn_rows).astype(jnp.bfloat16)
    normed = normalize(first_residual.astype(jnp.float32), attn_gain).astype(jnp.bfloat16)
    group_normed = lax.all_gather(normed, "tensor", axis=0, tiled=True)
    flat_ids = expert_ids.reshape(-1)
    onehot = (flat_ids[:, None] == jnp.arange(all_experts, dtype=jnp.int32)[None, :]).astype(
        jnp.int32
    )
    earlier = jnp.cumsum(onehot, axis=0) - onehot
    rank = jnp.sum(earlier * onehot, axis=1)
    dest = flat_ids * capacity + rank
    row_owner = jnp.arange(flat_ids.shape[0], dtype=jnp.int32) // TOP
    slot_row = jnp.full((all_experts * capacity,), group_rows, jnp.int32).at[dest].set(row_owner)
    slot_weight = (
        jnp.zeros((all_experts * capacity,), jnp.float32).at[dest].set(route_weights.reshape(-1))
    )
    own_slots = lax.dynamic_index_in_dim(
        slot_row.reshape(n_expert, 2, capacity), half, 1, keepdims=False
    )
    own_weights = lax.dynamic_index_in_dim(
        slot_weight.reshape(n_expert, 2, capacity), half, 1, keepdims=False
    )
    padded_rows = jnp.concatenate([group_normed, jnp.zeros((1, width), jnp.bfloat16)], axis=0)
    gate_w = w_gate[0]
    up_w = w_up[0]
    down_w = w_down[0]
    outgoing = jnp.take(padded_rows, own_slots, axis=0)
    arrived = lax.all_to_all(outgoing, "expert", split_axis=0, concat_axis=0, tiled=True)
    flat = arrived.reshape(-1, width)
    gate = jnp.dot(flat, gate_w, preferred_element_type=jnp.float32)
    up = jnp.dot(flat, up_w, preferred_element_type=jnp.float32)
    act = (jax.nn.silu(gate) * up).astype(jnp.bfloat16)
    part = jnp.dot(act, down_w, preferred_element_type=jnp.float32).astype(jnp.bfloat16)
    send_part = part.reshape(arrived.shape)
    returned = lax.all_to_all(send_part, "expert", split_axis=0, concat_axis=0, tiled=True)
    weighted = own_weights.reshape(-1)[:, None] * returned.reshape(-1, width).astype(jnp.float32)
    term = (
        jnp.zeros((group_rows + 1, width), jnp.float32)
        .at[own_slots.reshape(-1)]
        .add(weighted)[:group_rows]
    )
    expert_sum = lax.psum_scatter(
        term.astype(jnp.bfloat16), "tensor", scatter_dimension=0, tiled=True
    ).astype(jnp.float32)
    next_residual = (first_residual.astype(jnp.float32) + expert_sum).astype(jnp.bfloat16)
    own_normed = normalize(next_residual.astype(jnp.float32), input_gain).astype(jnp.bfloat16)
    next_normed = lax.all_gather(own_normed, "tensor", axis=0, tiled=True)
    query_cols = q_weight.shape[1]
    kv_cols = kv_weight.shape[1]
    query_raw = jnp.dot(
        next_normed,
        lax.all_gather(q_weight, "expert", axis=0, tiled=True),
        preferred_element_type=jnp.float32,
    )
    kv_raw = jnp.dot(
        next_normed,
        lax.all_gather(kv_weight, "expert", axis=0, tiled=True),
        preferred_element_type=jnp.float32,
    )
    head_size = q_gain.shape[0]
    queries = (
        normalize(query_raw.reshape(group_rows, -1, head_size), q_gain)
        .reshape(group_rows, query_cols)
        .astype(jnp.bfloat16)
    )
    heads_here = kv_cols // head_size
    head_number = tensor_index * heads_here + jnp.arange(heads_here, dtype=jnp.int32)
    is_key = head_number < KV_HEADS
    kv_shaped = kv_raw.reshape(group_rows, heads_here, head_size)
    keys_values = (
        jnp.where(is_key[None, :, None], normalize(kv_shaped, k_gain), kv_shaped)
        .reshape(group_rows, kv_cols)
        .astype(jnp.bfloat16)
    )
    return (next_residual, queries, keys_values)


def solution(mesh):
    return jax.shard_map(
        per_device,
        mesh=mesh,
        in_specs=(
            P("expert", "tensor"),
            P("tensor", None),
            P(("expert", "tensor"), None),
            P(),
            P("expert", None),
            P("expert", None),
            P("expert", None, "tensor"),
            P("expert", None, "tensor"),
            P("expert", "tensor", None),
            P(),
            P("expert", "tensor"),
            P("expert", "tensor"),
            P(),
            P(),
        ),
        out_specs=(P(("expert", "tensor"), None), P("expert", "tensor"), P("expert", "tensor")),
        check_vma=False,
    )
```

profile of v0, /device:TPU:2, one launch (start us, length us, event | category | flops | bytes accessed | tf_op | source)
XLA Modules:
  0.0 475.3 jit_solution(3789116620057749564)
XLA Ops:
  8.1 1.5 copy-done
  9.6 2.3 fusion.42
  13.4 4.3 scatter_custom_fusion
  18.4 0.7 fusion.40
  19.3 32.0 %reduce-scatter.3.cloned.1.call-done = f32[16,2048]{1,0:T(8,128)} async-done(((f32[128,2048]{1,0:T(8,128)}), f32[16,2048]{1,0:T(8,128)}) %reduce-scatter.3.cloned.1.call-update) | async-done | bytes 131088 | tf_op jit(solution)/shard_map/reduce_scatter | solution.py:40
  51.3 1.0 fusion.26
  52.4 13.8 %all_gather.12 = bf16[128,2048]{1,0:T(8,128)(2,1)S(1)} all-gather(bf16[16,2048]{1,0:T(8,128)(2,1)S(1)} %fusion.28), channel_id=1, replica_groups=mesh['expert'=64,'tensor'=8] {'tensor'}, dimensions={0}, use_global_device_ids=true | all-gather | bytes 589824 | tf_op jit(solution)/shard_map/all_gather | solution.py:48
  66.3 4.3 gather_fusion
  70.6 6.1 %reshape.208 = bf16[64,12,2048]{2,1,0:T(8,128)(2,1)} reshape(bf16[768,2048]{1,0:T(8,128)(2,1)} %gather_fusion) | data formatting | bytes 6291456 | tf_op jit(solution)/shard_map/jit(_take)/gather | solution.py:71
  76.6 2.6 broadcast_select_fusion
  79.3 111.8 %all_to_all.10 = bf16[64,12,2048]{2,1,0:T(8,128)(2,1)} all-to-all(bf16[64,12,2048]{2,1,0:T(8,128)(2,1)S(1)} %broadcast_select_fusion), channel_id=1, replica_groups=mesh['expert'=64,'tensor'=8] {'expert'}, dimensions={0} | all-to-all | bytes 6291456 | tf_op jit(solution)/shard_map/all_to_all | solution.py:72
  191.1 6.2 %reshape.204 = bf16[768,2048]{1,0:T(8,128)(2,1)} reshape(bf16[64,12,2048]{2,1,0:T(8,128)(2,1)} %all_to_all.10) | data formatting | bytes 6291456 | tf_op jit(solution)/shard_map/reshape | solution.py:73
  197.3 3.3 fusion.7
  200.5 6.5 %convolution_convert_fusion = bf16[768,2048]{1,0:T(8,128)(2,1)} fusion(bf16[768,2048]{1,0:T(8,128)(2,1)} %reshape.204, bf16[1,192,2048]{2,1,0:T(8,128)(2,1)} %param.22, bf16[1,2048,192]{1,2,0:T(8,128)(2,1)} %param.21, f32[768,192]{0,1:T(8,128)S(1)} %fusion.7), kind=kOutput, calls=%fused_computation.7 | convolution fusion | flops 1210417152 | bytes 8454144 | tf_op jit(solution)/shard_map/dot_general | solution.py:77
  207.0 6.1 %reshape.205 = bf16[64,12,2048]{2,1,0:T(8,128)(2,1)} reshape(bf16[768,2048]{1,0:T(8,128)(2,1)} %convolution_convert_fusion) | data formatting | bytes 6291456 | tf_op jit(solution)/shard_map/reshape | solution.py:78
  213.1 12.7 %all-to-all-start.1 = ((bf16[64,12,2048]{2,1,0:T(8,128)(2,1)}), bf16[64,12,2048]{2,1,0:T(8,128)(2,1)}, u32[]{:S(2)}, u32[]{:S(2)}) async-start(bf16[64,12,2048]{2,1,0:T(8,128)(2,1)} %reshape.205), calls=%async_computation.2 | async-start | bytes 8388608 | tf_op jit(solution)/shard_map/all_to_all | solution.py:79
  226.2 4.5 scatter_custom_fusion.1
  231.1 96.7 %all-to-all-done.1 = bf16[64,12,2048]{2,1,0:T(8,128)(2,1)} async-done(((bf16[64,12,2048]{2,1,0:T(8,128)(2,1)}), bf16[64,12,2048]{2,1,0:T(8,128)(2,1)}, u32[]{:S(2)}, u32[]{:S(2)}) %all-to-all-start.1) | async-done | bytes 3145760 | tf_op jit(solution)/shard_map/all_to_all | solution.py:79
  327.8 6.7 %reshape.206 = f32[768,2048]{1,0:T(8,128)} reshape(bf16[64,12,2048]{2,1,0:T(8,128)(2,1)} %all-to-all-done.1) | data formatting | bytes 9437184 | tf_op jit(solution)/shard_map/convert_element_type | solution.py:80
  334.5 15.8 %scatter_custom_fusion.2 = f32[129,2048]{1,0:T(8,128)S(1)} fusion(s32[768]{0:T(1024)S(1)} %fusion.37, f32[768,2048]{1,0:T(8,128)} %reshape.206, f32[768]{0:T(1024)S(1)} %mul.130, f32[]{:T(128)} %constant.76.clone.1), kind=kCustom, calls=%fused_computation.4 | custom fusion | flops 3145728 | bytes 7352324 | tf_op jit(solution)/shard_map/scatter-add | solution.py:84
  350.3 0.9 slice.20
  351.2 0.5 all-gather.2.cloned.1.call-update
  351.7 72.7 %all_gather.15 = bf16[2048,128]{1,0:T(8,128)(2,1)S(1)} all-gather(bf16[32,128]{1,0:T(8,128)(2,1)S(1)} %copy-done.4), channel_id=1, replica_groups=mesh['expert'=64,'tensor'=8] {'expert'}, dimensions={0}, use_global_device_ids=true | all-gather | bytes 532480 | tf_op jit(solution)/shard_map/all_gather | solution.py:101
  424.5 1.0 fusion.23
  425.6 13.1 %all_gather.13 = bf16[128,2048]{1,0:T(8,128)(2,1)S(1)} all-gather(bf16[16,2048]{1,0:T(8,128)(2,1)S(1)} %fusion.25), channel_id=1, replica_groups=mesh['expert'=64,'tensor'=8] {'tensor'}, dimensions={0}, use_global_device_ids=true | all-gather | bytes 589824 | tf_op jit(solution)/shard_map/all_gather | solution.py:91
  438.7 19.9 %all-gather.2.cloned.1.call-done = bf16[2048,512]{1,0:T(8,128)(2,1)} async-done(((bf16[32,512]{1,0:T(8,128)(2,1)}), bf16[2048,512]{1,0:T(8,128)(2,1)}) %all-gather.2.cloned.1.call-update) | async-done | bytes 2097168 | tf_op jit(solution)/shard_map/all_gather | solution.py:96
  458.6 2.8 fusion.41
  461.4 1.7 mul.146
  463.1 1.8 reduce_sum.51
  464.9 0.9 add_rsqrt_fusion
  466.2 0.7 copy.41
  467.1 0.7 fusion.21
  (64 shorter events, 3.9 us)
Async XLA Ops:
  8.0 1.6 copy-start
  8.0 4.0 copy-start.3
  8.0 43.2 %reduce-scatter.3.cloned.1.call-start = ((), (), s32[]{:S(2)}) async-start(), calls=%async_computation.4 | async-start | bytes 1179648 | tf_op jit(solution)/shard_map/reduce_scatter | solution.py:40
  11.9 39.3 %copy-start.2 = (bf16[16,2048]{1,0:T(8,128)(2,1)S(1)}, bf16[16,2048]{1,0:T(8,128)(2,1)}, u32[]{:S(2)}) copy-start(bf16[16,2048]{1,0:T(8,128)(2,1)} %param.16) | copy-start | bytes 196612
  11.9 40.4 %copy-start.5 = (f32[2048]{0:T(1024)S(1)}, f32[2048]{0:T(1024)}, u32[]{:S(2)}) copy-start(f32[2048]{0:T(1024)} %param.17) | copy-start | bytes 24580
  213.1 12.9 %copy-start.7 = (f32[128,8]{0,1:T(8,128)S(1)}, f32[128,8]{0,1:T(8,128)}, u32[]{:S(2)}) copy-start(f32[128,8]{0,1:T(8,128)} %param.19) | copy-start | bytes 12292
  213.1 114.7 %all-to-all-start.1 = ((bf16[64,12,2048]{2,1,0:T(8,128)(2,1)}), bf16[64,12,2048]{2,1,0:T(8,128)(2,1)}, u32[]{:S(2)}, u32[]{:S(2)}) async-start(bf16[64,12,2048]{2,1,0:T(8,128)(2,1)} %reshape.205), calls=%async_computation.2 | async-start | bytes 8388608 | tf_op jit(solution)/shard_map/all_to_all | solution.py:79
  225.8 198.7 %reduce-scatter.5.cloned.1.call-start = ((), (), s32[]{:S(2)}) async-start(), calls=%async_computation.5 | async-start | bytes 589824 | tf_op jit(solution)/shard_map/reduce_scatter | solution.py:86
  334.5 17.3 %copy-start.4 = (bf16[32,128]{1,0:T(8,128)(2,1)S(1)}, bf16[32,128]{1,0:T(8,128)(2,1)}, u32[]{:S(2)}) copy-start(bf16[32,128]{1,0:T(8,128)(2,1)} %param.25) | copy-start | bytes 24580
  334.5 90.0 %copy-start.9 = (f32[128]{0:T(128)S(1)}, f32[128]{0:T(128)}, u32[]{:S(2)}) copy-start(f32[128]{0:T(128)} %param.26) | copy-start | bytes 1540
  334.5 91.0 %copy-start.6 = (f32[2048]{0:T(1024)S(1)}, f32[2048]{0:T(1024)}, u32[]{:S(2)}) copy-start(f32[2048]{0:T(1024)} %param.23) | copy-start | bytes 24580
  351.1 107.4 %all-gather.2.cloned.1.call-start = ((), (), s32[]{:S(2)}) async-start(), calls=%async_computation.6 | async-start | bytes 2129920 | tf_op jit(solution)/shard_map/all_gather | solution.py:96
  424.5 41.6 %copy-start.8 = (f32[128]{0:T(128)S(1)}, f32[128]{0:T(128)}, u32[]{:S(2)}) copy-start(f32[128]{0:T(128)} %param.27) | copy-start | bytes 1540
  425.5 41.6 %copy-start.1 = (bf16[16,2048]{1,0:T(8,128)(2,1)}, bf16[16,2048]{1,0:T(8,128)(2,1)S(1)}, u32[]{:S(2)}) copy-start(bf16[16,2048]{1,0:T(8,128)(2,1)S(1)} %get-tuple-element.16) | copy-start | bytes 196612
Sparse Core Ops, SparseCore 0:
  12.1 39.1 reduce-scatter.2
  351.3 53.9 reduce-scatter.4
Sparse Core Ops, SparseCore 1:
  354.7 103.8 all-gather.1
where the time goes:
time: 476 us; the launch traced here: 475 us
  blocking collectives  211 us (44%)
  waiting for transfers between devices  149 us (31%)
  local copies, waits for them, and re-layouts  46 us (10%)
  other arithmetic  24.7 us (5%)
  between operations  15.8 us (3%)
  matrix products  15.2 us (3%)
  starting transfers between devices  12.9 us (3%)
    all_to_all x1, blocking collectives, per_device(): lax.all_to_all(outgoing, 'expert', split_axis=0, concat_axis=0, tiled=True)  112 us
    all_to_all x1, waiting for transfers between devices, per_device(): lax.all_to_all(send_part, 'expert', split_axis=0, concat_axis=0, tiled=True)  96.7 us
    all_gather x1, blocking collectives, per_device(): lax.all_gather(kv_weight, 'expert', axis=0, tiled=True)  72.7 us
    reduce_scatter x1, waiting for transfers between devices, per_device(): lax.psum_scatter(jnp.dot(attn_out, out_weight, preferred_element_type=jnp...  32 us
    all_gather x1, waiting for transfers between devices, per_device(): lax.all_gather(q_weight, 'expert', axis=0, tiled=True)  19.9 us
    scatter-add x1, other arithmetic, per_device(): term = jnp.zeros((group_rows + 1, width), jnp.float32).at[own_slots.resha...  15.8 us
    all_gather x1, blocking collectives, per_device(): group_normed = lax.all_gather(normed, 'tensor', axis=0, tiled=True)  13.8 us
    all_gather x1, blocking collectives, per_device(): next_normed = lax.all_gather(own_normed, 'tensor', axis=0, tiled=True)  13.1 us
  transfers between devices with their start and end apart: 4, of which 3 were waited for; matrix products, arithmetic and copies ran while one was open for 3% of the time, Pallas kernels for 0%

commit v1 on v0

--- a/solution.py
+++ b/solution.py
@@ -98,7 +98,9 @@
     )
     kv_raw = jnp.dot(
         next_normed,
-        lax.all_gather(kv_weight, "expert", axis=0, tiled=True),
+        jnp.concatenate(
+            lax.all_to_all(jnp.stack([kv_weight] * lax.axis_size("expert")), "expert", 0, 0), axis=0
+        ),
         preferred_element_type=jnp.float32,
     )
     head_size = q_gain.shape[0]

time: 476 us -> 477 us (level)
  blocking collectives: 211 us -> 139 us
  waiting for transfers between devices: 149 us -> 189 us
  starting transfers between devices: 12.9 us -> 44.3 us
    all_gather x1 -> x0, blocking collectives: 72.7 us -> none  [per_device(): lax.all_gather(kv_weight, 'expert', axis=0, tiled=True)]
    all_to_all x0 -> x1, starting transfers between devices: none -> 31.5 us  [per_device(): lax.all_to_all(jnp.stack([kv_weight] * lax.axis_size('expert')), 'expert'...]
    reduce_scatter x1, waiting for transfers between devices: 0.02 us -> 21.7 us  [per_device(): lax.psum_scatter(term.astype(jnp.bfloat16), 'tensor', scatter_dimension=0...]
    all_gather x1, waiting for transfers between devices: 19.9 us -> 38.4 us  [per_device(): lax.all_gather(q_weight, 'expert', axis=0, tiled=True)]
  transfers between devices with their start and end apart: 4 -> 5, of which waited for: 3 -> 4; matrix products, arithmetic and copies ran while one was open for 3% -> 4% of each run, Pallas kernels for 0% -> 0%
where the time goes in v1:
time: 477 us; the launch traced here: 476 us
  waiting for transfers between devices  189 us (40%)
  blocking collectives  139 us (29%)
  local copies, waits for them, and re-layouts  46.9 us (10%)
  starting transfers between devices  44.3 us (9%)
  other arithmetic  24.7 us (5%)
  between operations  15.9 us (3%)
  matrix products  15.2 us (3%)
    all_to_all x1, blocking collectives, per_device(): lax.all_to_all(outgoing, 'expert', split_axis=0, concat_axis=0, tiled=True)  112 us
    all_to_all x1, waiting for transfers between devices, per_device(): lax.all_to_all(send_part, 'expert', split_axis=0, concat_axis=0, tiled=True)  96.7 us
    all_gather x1, waiting for transfers between devices, per_device(): lax.all_gather(q_weight, 'expert', axis=0, tiled=True)  38.4 us
    reduce_scatter x1, waiting for transfers between devices, per_device(): lax.psum_scatter(jnp.dot(attn_out, out_weight, preferred_element_type=jnp...  32 us
    all_to_all x1, starting transfers between devices, per_device(): lax.all_to_all(jnp.stack([kv_weight] * lax.axis_size('expert')), 'expert'...  31.5 us
    reduce_scatter x1, waiting for transfers between devices, per_device(): lax.psum_scatter(term.astype(jnp.bfloat16), 'tensor', scatter_dimension=0...  21.7 us
    scatter-add x1, other arithmetic, per_device(): term = jnp.zeros((group_rows + 1, width), jnp.float32).at[own_slots.resha...  15.8 us
    all_gather x1, blocking collectives, per_device(): group_normed = lax.all_gather(normed, 'tensor', axis=0, tiled=True)  13.8 us
  transfers between devices with their start and end apart: 5, of which 4 were waited for; matrix products, arithmetic and copies ran while one was open for 4% of the time, Pallas kernels for 0%

profile of v1, /device:TPU:2, one launch (start us, length us, event | category | flops | bytes accessed | tf_op | source)
XLA Modules:
  0.0 475.7 jit_solution(13633351539413089812)
XLA Ops:
  8.1 1.5 copy-done
  9.6 2.3 fusion.42
  13.4 4.3 scatter_custom_fusion
  18.4 0.7 fusion.40
  19.3 32.0 %reduce-scatter.3.cloned.1.call-done = f32[16,2048]{1,0:T(8,128)} async-done(((f32[128,2048]{1,0:T(8,128)}), f32[16,2048]{1,0:T(8,128)}) %reduce-scatter.3.cloned.1.call-update) | async-done | bytes 131088 | tf_op jit(solution)/shard_map/reduce_scatter | solution.py:40
  51.3 1.0 fusion.26
  52.4 13.8 %all_gather.9 = bf16[128,2048]{1,0:T(8,128)(2,1)S(1)} all-gather(bf16[16,2048]{1,0:T(8,128)(2,1)S(1)} %fusion.28), channel_id=1, replica_groups=mesh['expert'=64,'tensor'=8] {'tensor'}, dimensions={0}, use_global_device_ids=true | all-gather | bytes 589824 | tf_op jit(solution)/shard_map/all_gather | solution.py:48
  66.3 4.3 gather_fusion
  70.6 6.1 %reshape.214 = bf16[64,12,2048]{2,1,0:T(8,128)(2,1)} reshape(bf16[768,2048]{1,0:T(8,128)(2,1)} %gather_fusion) | data formatting | bytes 6291456 | tf_op jit(solution)/shard_map/jit(_take)/gather | solution.py:71
  76.6 2.6 broadcast_select_fusion
  79.3 111.8 %all_to_all.15 = bf16[64,12,2048]{2,1,0:T(8,128)(2,1)} all-to-all(bf16[64,12,2048]{2,1,0:T(8,128)(2,1)S(1)} %broadcast_select_fusion), channel_id=1, replica_groups=mesh['expert'=64,'tensor'=8] {'expert'}, dimensions={0} | all-to-all | bytes 6291456 | tf_op jit(solution)/shard_map/all_to_all | solution.py:72
  191.1 6.2 %reshape.209 = bf16[768,2048]{1,0:T(8,128)(2,1)} reshape(bf16[64,12,2048]{2,1,0:T(8,128)(2,1)} %all_to_all.15) | data formatting | bytes 6291456 | tf_op jit(solution)/shard_map/reshape | solution.py:73
  197.3 3.3 fusion.7
  200.5 6.5 %convolution_convert_fusion = bf16[768,2048]{1,0:T(8,128)(2,1)} fusion(bf16[768,2048]{1,0:T(8,128)(2,1)} %reshape.209, bf16[1,192,2048]{2,1,0:T(8,128)(2,1)} %param.22, bf16[1,2048,192]{1,2,0:T(8,128)(2,1)} %param.21, f32[768,192]{0,1:T(8,128)S(1)} %fusion.7), kind=kOutput, calls=%fused_computation.7 | convolution fusion | flops 1210417152 | bytes 8454144 | tf_op jit(solution)/shard_map/dot_general | solution.py:77
  207.0 6.1 %reshape.210 = bf16[64,12,2048]{2,1,0:T(8,128)(2,1)} reshape(bf16[768,2048]{1,0:T(8,128)(2,1)} %convolution_convert_fusion) | data formatting | bytes 6291456 | tf_op jit(solution)/shard_map/reshape | solution.py:78
  213.1 12.7 %all-to-all-start.1 = ((bf16[64,12,2048]{2,1,0:T(8,128)(2,1)}), bf16[64,12,2048]{2,1,0:T(8,128)(2,1)}, u32[]{:S(2)}, u32[]{:S(2)}) async-start(bf16[64,12,2048]{2,1,0:T(8,128)(2,1)} %reshape.210), calls=%async_computation.2 | async-start | bytes 8388608 | tf_op jit(solution)/shard_map/all_to_all | solution.py:79
  226.2 4.5 scatter_custom_fusion.1
  231.1 96.7 %all-to-all-done.1 = bf16[64,12,2048]{2,1,0:T(8,128)(2,1)} async-done(((bf16[64,12,2048]{2,1,0:T(8,128)(2,1)}), bf16[64,12,2048]{2,1,0:T(8,128)(2,1)}, u32[]{:S(2)}, u32[]{:S(2)}) %all-to-all-start.1) | async-done | bytes 3145760 | tf_op jit(solution)/shard_map/all_to_all | solution.py:79
  327.8 6.7 %reshape.212 = f32[768,2048]{1,0:T(8,128)} reshape(bf16[64,12,2048]{2,1,0:T(8,128)(2,1)} %all-to-all-done.1) | data formatting | bytes 9437184 | tf_op jit(solution)/shard_map/convert_element_type | solution.py:80
  334.5 15.8 %scatter_custom_fusion.2 = f32[129,2048]{1,0:T(8,128)S(1)} fusion(s32[768]{0:T(1024)S(1)} %fusion.37, f32[768,2048]{1,0:T(8,128)} %reshape.212, f32[768]{0:T(1024)S(1)} %mul.130, f32[]{:T(128)} %constant.76.clone.1), kind=kCustom, calls=%fused_computation.4 | custom fusion | flops 3145728 | bytes 7352324 | tf_op jit(solution)/shard_map/scatter-add | solution.py:84
  350.3 0.9 slice.20
  351.8 0.9 stack.2
  352.6 31.5 %all-to-all-start.2 = ((bf16[64,32,128]{2,1,0:T(8,128)(2,1)}), bf16[64,32,128]{2,1,0:T(8,128)(2,1)S(1)}, u32[]{:S(2)}, u32[]{:S(2)}) async-start(bf16[64,32,128]{2,1,0:T(8,128)(2,1)} %stack.2), calls=%async_computation.4 | async-start | bytes 1048576 | tf_op jit(solution)/shard_map/all_to_all | solution.py:102
  384.1 21.7 %reduce-scatter.5.cloned.1.call-done = bf16[16,2048]{1,0:T(8,128)(2,1)} async-done(((bf16[128,2048]{1,0:T(8,128)(2,1)}), bf16[16,2048]{1,0:T(8,128)(2,1)}) %reduce-scatter.5.cloned.1.call-update) | async-done | bytes 65552 | tf_op jit(solution)/shard_map/reduce_scatter | solution.py:86
  405.8 1.0 fusion.23
  406.9 13.7 %all_gather.10 = bf16[128,2048]{1,0:T(8,128)(2,1)S(1)} all-gather(bf16[16,2048]{1,0:T(8,128)(2,1)S(1)} %fusion.25), channel_id=1, replica_groups=mesh['expert'=64,'tensor'=8] {'tensor'}, dimensions={0}, use_global_device_ids=true | all-gather | bytes 589824 | tf_op jit(solution)/shard_map/all_gather | solution.py:91
  420.6 38.4 %all-gather.2.cloned.1.call-done = bf16[2048,512]{1,0:T(8,128)(2,1)} async-done(((bf16[32,512]{1,0:T(8,128)(2,1)}), bf16[2048,512]{1,0:T(8,128)(2,1)}) %all-gather.2.cloned.1.call-update) | async-done | bytes 2097168 | tf_op jit(solution)/shard_map/all_gather | solution.py:96
  459.1 2.7 fusion.41
  461.8 1.7 mul.146
  463.5 1.8 reduce_sum.51
  465.3 0.9 add_rsqrt_fusion
  466.7 0.7 copy.41
  (66 shorter events, 5.1 us)
Async XLA Ops:
  8.0 1.6 copy-start
  8.0 4.0 copy-start.3
  8.0 43.2 %reduce-scatter.3.cloned.1.call-start = ((), (), s32[]{:S(2)}) async-start(), calls=%async_computation.5 | async-start | bytes 1179648 | tf_op jit(solution)/shard_map/reduce_scatter | solution.py:40
  11.9 39.3 %copy-start.2 = (bf16[16,2048]{1,0:T(8,128)(2,1)S(1)}, bf16[16,2048]{1,0:T(8,128)(2,1)}, u32[]{:S(2)}) copy-start(bf16[16,2048]{1,0:T(8,128)(2,1)} %param.16) | copy-start | bytes 196612
  11.9 40.4 %copy-start.5 = (f32[2048]{0:T(1024)S(1)}, f32[2048]{0:T(1024)}, u32[]{:S(2)}) copy-start(f32[2048]{0:T(1024)} %param.17) | copy-start | bytes 24580
  213.1 12.9 %copy-start.7 = (f32[128,8]{0,1:T(8,128)S(1)}, f32[128,8]{0,1:T(8,128)}, u32[]{:S(2)}) copy-start(f32[128,8]{0,1:T(8,128)} %param.19) | copy-start | bytes 12292
  213.1 114.7 %all-to-all-start.1 = ((bf16[64,12,2048]{2,1,0:T(8,128)(2,1)}), bf16[64,12,2048]{2,1,0:T(8,128)(2,1)}, u32[]{:S(2)}, u32[]{:S(2)}) async-start(bf16[64,12,2048]{2,1,0:T(8,128)(2,1)} %reshape.210), calls=%async_computation.2 | async-start | bytes 8388608 | tf_op jit(solution)/shard_map/all_to_all | solution.py:79
  225.8 180.0 %reduce-scatter.5.cloned.1.call-start = ((), (), s32[]{:S(2)}) async-start(), calls=%async_computation.6 | async-start | bytes 589824 | tf_op jit(solution)/shard_map/reduce_scatter | solution.py:86
  334.5 17.3 %copy-start.4 = (bf16[32,128]{1,0:T(8,128)(2,1)S(1)}, bf16[32,128]{1,0:T(8,128)(2,1)}, u32[]{:S(2)}) copy-start(bf16[32,128]{1,0:T(8,128)(2,1)} %param.25) | copy-start | bytes 24580
  350.2 33.9 %copy-start.9 = (f32[128]{0:T(128)S(1)}, f32[128]{0:T(128)}, u32[]{:S(2)}) copy-start(f32[128]{0:T(128)} %param.26) | copy-start | bytes 1540
  350.3 56.6 %copy-start.6 = (f32[2048]{0:T(1024)S(1)}, f32[2048]{0:T(1024)}, u32[]{:S(2)}) copy-start(f32[2048]{0:T(1024)} %param.23) | copy-start | bytes 24580
  351.2 107.9 %all-gather.2.cloned.1.call-start = ((), (), s32[]{:S(2)}) async-start(), calls=%async_computation.7 | async-start | bytes 2129920 | tf_op jit(solution)/shard_map/all_gather | solution.py:96
  352.6 113.6 %all-to-all-start.2 = ((bf16[64,32,128]{2,1,0:T(8,128)(2,1)}), bf16[64,32,128]{2,1,0:T(8,128)(2,1)S(1)}, u32[]{:S(2)}, u32[]{:S(2)}) async-start(bf16[64,32,128]{2,1,0:T(8,128)(2,1)} %stack.2), calls=%async_computation.4 | async-start | bytes 1048576 | tf_op jit(solution)/shard_map/all_to_all | solution.py:102
  384.1 82.5 %copy-start.8 = (f32[128]{0:T(128)S(1)}, f32[128]{0:T(128)}, u32[]{:S(2)}) copy-start(f32[128]{0:T(128)} %param.27) | copy-start | bytes 1540
  406.8 60.8 %copy-start.1 = (bf16[16,2048]{1,0:T(8,128)(2,1)}, bf16[16,2048]{1,0:T(8,128)(2,1)S(1)}, u32[]{:S(2)}) copy-start(bf16[16,2048]{1,0:T(8,128)(2,1)S(1)} %get-tuple-element.16) | copy-start | bytes 196612
Sparse Core Ops, SparseCore 0:
  12.1 39.1 reduce-scatter.2
  351.3 54.4 reduce-scatter.4
Sparse Core Ops, SparseCore 1:
  354.7 104.3 all-gather.1
